TPU v7x, 32 devices: a whole 2x2x4 slice. The times are simulated.
32 devices in a mesh: fsdp: 8 (over y, x, core), seq: 4 (over z).
Axes of the slice: x: 2, y: 2, z: 4, core: 2. Of those that a mesh axis runs over, the one named last changes fastest.
Arguments:
- hidden_in: bfloat16 [8, 1024, 2048], P('fsdp', 'seq'), may hold values from -6 to 6
- lengths: int32 [8], P('fsdp'), may hold values from 512 to 1024, as said below
- cotangent: bfloat16 [8, 1024, 2048], P('fsdp', 'seq'), may hold values from -6 to 6
- in_weight: bfloat16 [2048, 6144], P(('fsdp', 'seq')), may hold values from -0.125 to 0.125
- in_bias: bfloat16 [6144], P(('fsdp', 'seq')), may hold values from -0.29882812 to 0.29882812
- out_weight: bfloat16 [2048, 2048], P(('fsdp', 'seq')), may hold values from -1 to 1
- out_bias: bfloat16 [2048], P(('fsdp', 'seq')), may hold values from -2 to 2
- up_weight: bfloat16 [8192, 2048], P(('fsdp', 'seq')), may hold values from -0.125 to 0.125
- up_bias: bfloat16 [8192], P(('fsdp', 'seq')), may hold values from -2 to 2
- down_weight: bfloat16 [8192, 2048], P(('fsdp', 'seq')), may hold values from -0.0625 to 0.0625
- down_bias: bfloat16 [2048], P(('fsdp', 'seq')), may hold values from -2 to 2
- first_gain: bfloat16 [2048], P(('fsdp', 'seq')), may hold values from 0.5 to 1.5
- first_shift: bfloat16 [2048], P(('fsdp', 'seq')), may hold values from -2 to 2
- second_gain: bfloat16 [2048], P(('fsdp', 'seq')), may hold values from 0.5 to 1.5
- second_shift: bfloat16 [2048], P(('fsdp', 'seq')), may hold values from -2 to 2
Outputs:
- layer_output: float32 [8, 1024, 2048], P('fsdp', 'seq')
- input_gradient: float32 [8, 1024, 2048], P('fsdp', 'seq')
- in_weight_gradient: float32 [2048, 6144], P(('fsdp', 'seq'))
- in_bias_gradient: float32 [6144], P(('fsdp', 'seq'))
- out_weight_gradient: float32 [2048, 2048], P(('fsdp', 'seq'))
- out_bias_gradient: float32 [2048], P(('fsdp', 'seq'))
- up_weight_gradient: float32 [8192, 2048], P(('fsdp', 'seq'))
- up_bias_gradient: float32 [8192], P(('fsdp', 'seq'))
- down_weight_gradient: float32 [8192, 2048], P(('fsdp', 'seq'))
- down_bias_gradient: float32 [2048], P(('fsdp', 'seq'))
- first_gain_gradient: float32 [2048], P(('fsdp', 'seq'))
- first_shift_gradient: float32 [2048], P(('fsdp', 'seq'))
- second_gain_gradient: float32 [2048], P(('fsdp', 'seq'))
- second_shift_gradient: float32 [2048], P(('fsdp', 'seq'))
Inputs may be any that keep to these rules, and one draw needn't show every extreme that they name: `lengths`: tokens in use at the front of each slot; in every draw one slot is full and one holds 512 tokens.
All inputs are finite; a program needn't handle non-finite values.
Results may differ from a plain program's by a relative error of at most 0.014.
Values may be sent and summed in bfloat16 or wider, within the bound.
No kernel may reach another device: no remote copies, remote signals or barrier semaphores. Data moves between devices by JAX's collectives and lax.ppermute only.
A program may use at most 384 MiB of HBM per device.

v0:
```python
import jax
import jax.numpy as jnp
from jax import lax
from jax.sharding import PartitionSpec as P

HEADS = 16
HEAD_DIM = 128
ROT = 32
EPSILON = 1e-05
MASKED_SCORE = -1e30


def layer_norm(values, norm_gain, norm_shift):
    centred = values - jnp.mean(values, axis=-1, keepdims=True)
    spread = jnp.mean(centred * centred, axis=-1, keepdims=True)
    return centred * lax.rsqrt(spread + EPSILON) * norm_gain + norm_shift


def rotary_tables(positions):
    halves = jnp.arange(ROT // 2, dtype=jnp.float32)
    frequency = 1.0 / 10000.0 ** (halves * 2.0 / ROT)
    angles = positions.astype(jnp.float32)[:, None] * frequency[None, :]
    angles = jnp.concatenate([angles, angles], axis=1)
    return (jnp.cos(angles), jnp.sin(angles))


def rotate(values, cosine_table, sine_table):
    leading = values[..., :ROT]
    middle = ROT // 2
    turned = jnp.concatenate([-leading[..., middle:], leading[..., :middle]], axis=-1)
    leading = leading * cosine_table[:, None, :] + turned * sine_table[:, None, :]
    return jnp.concatenate([leading, values[..., ROT:]], axis=-1)


def exact_gelu(values):
    return jax.nn.gelu(values, approximate=False)


def matmul(left_side, right_side):
    return jnp.dot(left_side, right_side, preferred_element_type=jnp.float32)


def times_transposed(left_side, right_side):
    return lax.dot_general(
        left_side, right_side, (((1,), (1,)), ((), ())), preferred_element_type=jnp.float32
    )


def transposed_times(left_side, right_side):
    return lax.dot_general(
        left_side, right_side, (((0,), (0,)), ((), ())), preferred_element_type=jnp.float32
    )


def attend_slot(query, key_rows, value_rows, keep_mask):
    length_full = query.shape[0]
    block_rows = min(512, length_full)
    block_count = length_full // block_rows
    columns = jnp.arange(length_full, dtype=jnp.int32)
    scale_factor = HEAD_DIM ** (-0.5)

    def one_block(first_row):
        row_index = first_row + jnp.arange(block_rows, dtype=jnp.int32)
        query_block = lax.dynamic_slice_in_dim(query, first_row, block_rows, 0)
        scores = (
            jnp.einsum("qhd,khd->hqk", query_block, key_rows, preferred_element_type=jnp.float32)
            * scale_factor
        )
        allowed = (columns[None, :] <= row_index[:, None]) & keep_mask[None, :]
        scores = jnp.where(allowed[None], scores, MASKED_SCORE)
        largest = jnp.max(scores, axis=-1, keepdims=True)
        weights = jnp.exp(scores - largest)
        totals = jnp.sum(weights, axis=-1, keepdims=True)
        probabilities = (weights / totals).astype(jnp.bfloat16)
        mixed = jnp.einsum(
            "hqk,khd->qhd", probabilities, value_rows, preferred_element_type=jnp.float32
        )
        return (mixed, (largest + jnp.log(totals))[..., 0])

    starts = jnp.arange(block_count, dtype=jnp.int32) * block_rows
    mixed, log_sums = lax.map(one_block, starts)
    return (mixed.reshape(length_full, query.shape[1], query.shape[2]), log_sums)


def attend_slot_back(query, key_rows, value_rows, keep_mask, log_sums, mixed_delta):
    length_full = query.shape[0]
    block_rows = min(512, length_full)
    block_count = length_full // block_rows
    columns = jnp.arange(length_full, dtype=jnp.int32)
    scale_factor = HEAD_DIM ** (-0.5)

    def one_block(carried, member):
        key_delta, value_delta = carried
        first_row, log_block = member
        row_index = first_row + jnp.arange(block_rows, dtype=jnp.int32)
        query_block = lax.dynamic_slice_in_dim(query, first_row, block_rows, 0)
        delta_block = lax.dynamic_slice_in_dim(mixed_delta, first_row, block_rows, 0)
        scores = (
            jnp.einsum("qhd,khd->hqk", query_block, key_rows, preferred_element_type=jnp.float32)
            * scale_factor
        )
        allowed = (columns[None, :] <= row_index[:, None]) & keep_mask[None, :]
        scores = jnp.where(allowed[None], scores, MASKED_SCORE)
        probabilities = jnp.where(allowed[None], jnp.exp(scores - log_block[..., None]), 0.0)
        prob_delta = jnp.einsum(
            "qhd,khd->hqk", delta_block, value_rows, preferred_element_type=jnp.float32
        )
        row_dot = jnp.sum(probabilities * prob_delta, axis=-1, keepdims=True)
        score_delta = (probabilities * (prob_delta - row_dot)).astype(jnp.bfloat16)
        query_delta = (
            jnp.einsum("hqk,khd->qhd", score_delta, key_rows, preferred_element_type=jnp.float32)
            * scale_factor
        )
        key_delta = (
            key_delta
            + jnp.einsum(
                "hqk,qhd->khd", score_delta, query_block, preferred_element_type=jnp.float32
            )
            * scale_factor
        )
        value_delta = value_delta + jnp.einsum(
            "hqk,qhd->khd",
            probabilities.astype(jnp.bfloat16),
            delta_block,
            preferred_element_type=jnp.float32,
        )
        return ((key_delta, value_delta), query_delta)

    starts = jnp.arange(block_count, dtype=jnp.int32) * block_rows
    zeroes = jnp.zeros(query.shape, jnp.float32)
    (key_delta, value_delta), query_delta = lax.scan(
        one_block, (zeroes, zeroes), (starts, log_sums)
    )
    return (query_delta.reshape(query.shape), key_delta, value_delta)


def feed_forward(inner_in, up_matrix, up_offset, down_matrix):
    hidden_pre = times_transposed(inner_in, up_matrix) + up_offset.astype(jnp.float32)
    hidden_act, pull_act = jax.vjp(exact_gelu, hidden_pre)
    hidden_low = hidden_act.astype(jnp.bfloat16)
    return (hidden_low, pull_act, matmul(hidden_low, down_matrix))


def feed_back(inner_in, hidden_low, pull_act, delta_rows, up_matrix, down_matrix):
    delta_down = transposed_times(hidden_low, delta_rows)
    delta_pre = pull_act(times_transposed(delta_rows, down_matrix))[0].astype(jnp.bfloat16)
    delta_up = transposed_times(delta_pre, inner_in)
    delta_up_bias = jnp.sum(delta_pre.astype(jnp.float32), axis=0)
    delta_inner = matmul(delta_pre, up_matrix)
    return (delta_up, delta_up_bias, delta_down, delta_inner)


def local(
    hidden_in,
    lengths,
    cotangent,
    in_weight,
    in_bias,
    out_weight,
    out_bias,
    up_weight,
    up_bias,
    down_weight,
    down_bias,
    first_gain,
    first_shift,
    second_gain,
    second_shift,
):
    slot_count, token_count, width = hidden_in.shape
    seq_count = lax.axis_size("seq")
    seq_index = lax.axis_index("seq")
    length_full = token_count * seq_count
    row_count = slot_count * token_count
    (
        in_matrix,
        in_offset,
        out_matrix,
        out_offset,
        gain_one,
        shift_one,
        gain_two,
        shift_two,
        down_offset,
    ) = (
        lax.all_gather(in_weight, ("fsdp", "seq"), axis=0, tiled=True),
        lax.all_gather(in_bias, ("fsdp", "seq"), axis=0, tiled=True),
        lax.all_gather(out_weight, ("fsdp", "seq"), axis=0, tiled=True),
        lax.all_gather(out_bias, ("fsdp", "seq"), axis=0, tiled=True),
        lax.all_gather(first_gain, ("fsdp", "seq"), axis=0, tiled=True),
        lax.all_gather(first_shift, ("fsdp", "seq"), axis=0, tiled=True),
        lax.all_gather(second_gain, ("fsdp", "seq"), axis=0, tiled=True),
        lax.all_gather(second_shift, ("fsdp", "seq"), axis=0, tiled=True),
        lax.all_gather(down_bias, ("fsdp", "seq"), axis=0, tiled=True),
    )
    positions = seq_index * token_count + jnp.arange(token_count, dtype=jnp.int32)
    keep_local = positions[None, :] < lengths[:, None]
    keep_full = jnp.arange(length_full, dtype=jnp.int32)[None, :] < lengths[:, None]
    source = hidden_in.astype(jnp.float32)
    normed_one, pull_one = jax.vjp(
        layer_norm, source, gain_one.astype(jnp.float32), shift_one.astype(jnp.float32)
    )
    first_in = normed_one.astype(jnp.bfloat16).reshape(row_count, width)
    cosine_table, sine_table = rotary_tables(positions)
    joined = matmul(first_in, in_matrix) + in_offset.astype(jnp.float32)
    joined = joined.reshape(slot_count, token_count, 3, HEADS, HEAD_DIM)

    def rotate_both(query_part, key_part):
        return (
            rotate(query_part, cosine_table, sine_table),
            rotate(key_part, cosine_table, sine_table),
        )

    turned, pull_turn = jax.vjp(rotate_both, joined[:, :, 0], joined[:, :, 1])
    query, key_rows, value_rows = (
        lax.all_to_all(
            turned[0].astype(jnp.bfloat16), "seq", split_axis=2, concat_axis=1, tiled=True
        ),
        lax.all_to_all(
            turned[1].astype(jnp.bfloat16), "seq", split_axis=2, concat_axis=1, tiled=True
        ),
        lax.all_to_all(
            joined[:, :, 2].astype(jnp.bfloat16), "seq", split_axis=2, concat_axis=1, tiled=True
        ),
    )
    mixed_heads, log_sums = jax.vmap(attend_slot)(query, key_rows, value_rows, keep_full)
    mixed = lax.all_to_all(
        mixed_heads.astype(jnp.bfloat16), "seq", split_axis=1, concat_axis=2, tiled=True
    ).reshape(row_count, width)
    attn_branch = matmul(mixed, out_matrix) + out_offset.astype(jnp.float32)
    normed_two, pull_two = jax.vjp(
        layer_norm, source, gain_two.astype(jnp.float32), shift_two.astype(jnp.float32)
    )
    second_in = normed_two.astype(jnp.bfloat16)
    delta_out = jnp.where(keep_local[..., None], cotangent.astype(jnp.float32), 0.0)
    delta_low = delta_out.astype(jnp.bfloat16)
    delta_rows = delta_low.reshape(row_count, width)
    up_matrix, up_offset, down_matrix = (
        lax.all_gather(up_weight, "fsdp", axis=0, tiled=True),
        lax.all_gather(up_bias, "fsdp", axis=0, tiled=True),
        lax.all_gather(down_weight, "fsdp", axis=0, tiled=True),
    )
    inner_in = lax.all_gather(second_in, "seq", axis=1, tiled=True).reshape(
        slot_count * length_full, width
    )
    hidden_low, pull_act, branch_part = feed_forward(inner_in, up_matrix, up_offset, down_matrix)
    branch_sum = lax.psum_scatter(
        branch_part.reshape(slot_count, length_full, width).astype(jnp.bfloat16),
        "seq",
        scatter_dimension=1,
        tiled=True,
    ).astype(jnp.float32)
    mlp_branch = branch_sum + down_offset.astype(jnp.float32)
    delta_all = lax.all_gather(delta_low, "seq", axis=1, tiled=True).reshape(
        slot_count * length_full, width
    )
    delta_up, delta_up_bias, delta_down, delta_inner = feed_back(
        inner_in, hidden_low, pull_act, delta_all, up_matrix, down_matrix
    )
    second_delta = lax.psum_scatter(
        delta_inner.reshape(slot_count, length_full, width).astype(jnp.bfloat16),
        "seq",
        scatter_dimension=1,
        tiled=True,
    ).astype(jnp.float32)
    up_gradient, up_bias_gradient, down_gradient = (
        lax.psum_scatter(
            delta_up.astype(jnp.bfloat16), "fsdp", scatter_dimension=0, tiled=True
        ).astype(jnp.float32),
        lax.psum_scatter(
            delta_up_bias.astype(jnp.bfloat16), "fsdp", scatter_dimension=0, tiled=True
        ).astype(jnp.float32),
        lax.psum_scatter(
            delta_down.astype(jnp.bfloat16), "fsdp", scatter_dimension=0, tiled=True
        ).astype(jnp.float32),
    )
    layer_output = jnp.where(
        keep_local[..., None],
        source + attn_branch.reshape(slot_count, token_count, width) + mlp_branch,
        0.0,
    )
    source_two, gain_two_delta, shift_two_delta = pull_two(second_delta)
    bias_sum = jnp.sum(delta_out.reshape(row_count, width), axis=0)
    out_delta = transposed_times(mixed, delta_rows)
    mixed_delta = times_transposed(delta_rows, out_matrix).astype(jnp.bfloat16)
    mixed_delta = lax.all_to_all(
        mixed_delta.reshape(slot_count, token_count, HEADS, HEAD_DIM),
        "seq",
        split_axis=2,
        concat_axis=1,
        tiled=True,
    )
    query_delta, key_delta, value_delta = jax.vmap(attend_slot_back)(
        query, key_rows, value_rows, keep_full, log_sums, mixed_delta
    )
    query_back, key_back, value_back = (
        lax.all_to_all(
            query_delta.astype(jnp.bfloat16), "seq", split_axis=1, concat_axis=2, tiled=True
        ),
        lax.all_to_all(
            key_delta.astype(jnp.bfloat16), "seq", split_axis=1, concat_axis=2, tiled=True
        ),
        lax.all_to_all(
            value_delta.astype(jnp.bfloat16), "seq", split_axis=1, concat_axis=2, tiled=True
        ),
    )
    query_plain, key_plain = pull_turn(
        (query_back.astype(jnp.float32), key_back.astype(jnp.float32))
    )
    joined_delta = jnp.stack([query_plain, key_plain, value_back.astype(jnp.float32)], axis=2)
    joined_delta = joined_delta.reshape(row_count, 3 * width).astype(jnp.bfloat16)
    in_delta = transposed_times(first_in, joined_delta)
    in_bias_delta = jnp.sum(joined_delta.astype(jnp.float32), axis=0)
    first_delta = times_transposed(joined_delta, in_matrix).reshape(slot_count, token_count, width)
    source_one, gain_one_delta, shift_one_delta = pull_one(first_delta)
    (
        in_gradient,
        in_bias_gradient,
        out_gradient,
        bias_gradient,
        gain_one_gradient,
        shift_one_gradient,
        gain_two_gradient,
        shift_two_gradient,
    ) = (
        lax.psum_scatter(in_delta, ("fsdp", "seq"), scatter_dimension=0, tiled=True),
        lax.psum_scatter(in_bias_delta, ("fsdp", "seq"), scatter_dimension=0, tiled=True),
        lax.psum_scatter(out_delta, ("fsdp", "seq"), scatter_dimension=0, tiled=True),
        lax.psum_scatter(bias_sum, ("fsdp", "seq"), scatter_dimension=0, tiled=True),
        lax.psum_scatter(gain_one_delta, ("fsdp", "seq"), scatter_dimension=0, tiled=True),
        lax.psum_scatter(shift_one_delta, ("fsdp", "seq"), scatter_dimension=0, tiled=True),
        lax.psum_scatter(gain_two_delta, ("fsdp", "seq"), scatter_dimension=0, tiled=True),
        lax.psum_scatter(shift_two_delta, ("fsdp", "seq"), scatter_dimension=0, tiled=True),
    )
    input_gradient = delta_out + source_one + source_two
    return (
        layer_output,
        input_gradient,
        in_gradient,
        in_bias_gradient,
        out_gradient,
        bias_gradient,
        up_gradient,
        up_bias_gradient,
        down_gradient,
        bias_gradient,
        gain_one_gradient,
        shift_one_gradient,
        gain_two_gradient,
        shift_two_gradient,
    )


def solution(mesh):
    return jax.shard_map(
        local,
        mesh=mesh,
        in_specs=(
            P("fsdp", "seq", None),
            P("fsdp"),
            P("fsdp", "seq", None),
            P(("fsdp", "seq"), None),
            P(("fsdp", "seq")),
            P(("fsdp", "seq"), None),
            P(("fsdp", "seq")),
            P(("fsdp", "seq"), None),
            P(("fsdp", "seq")),
            P(("fsdp", "seq"), None),
            P(("fsdp", "seq")),
            P(("fsdp", "seq")),
            P(("fsdp", "seq")),
            P(("fsdp", "seq")),
            P(("fsdp", "seq")),
        ),
        out_specs=(
            P("fsdp", "seq", None),
            P("fsdp", "seq", None),
            P(("fsdp", "seq"), None),
            P(("fsdp", "seq")),
            P(("fsdp", "seq"), None),
            P(("fsdp", "seq")),
            P(("fsdp", "seq"), None),
            P(("fsdp", "seq")),
            P(("fsdp", "seq"), None),
            P(("fsdp", "seq")),
            P(("fsdp", "seq")),
            P(("fsdp", "seq")),
            P(("fsdp", "seq")),
            P(("fsdp", "seq")),
        ),
        check_vma=False,
    )
```

profile of v0, /device:TPU:0, one launch (start us, length us, event | category | flops | bytes accessed | tf_op | source)
XLA Modules:
  0.0 1959.2 jit_solution(5670677345125691977)
XLA Ops:
  16.4 43.3 %all-reduce.25 = (bf16[6144]{0:T(1024)(128)(2,1)S(1)}, bf16[2048]{0:T(1024)(128)(2,1)S(1)}, bf16[2048]{0:T(1024)(128)(2,1)S(1)}, bf16[2048]{0:T(1024)(128)(2,1)S...) all-reduce(bf16[6144]{0:T(1024)(128)(2,1)S(1)} %dynamic-update-slic, ...), channel_id=1, replica_groups=mesh['fsdp'=8,'seq'=4] {'fsdp','seq'}, use_global_device_ids=true, to_apply=%add.12 | all-reduce | flops 18432 | bytes 73728
  59.7 2.7 fusion.76
  67.0 9.8 all-gather
  76.8 66.3 %all-gather.12.cloned.1.call-done = bf16[1,1024,2048]{2,1,0:T(8,128)(2,1)} async-done(((bf16[1,256,2048]{2,1,0:T(8,128)(2,1)}), bf16[1,1024,2048]{2,1,0:T(8,128)(2,1)}) %all-gather.12.cloned.1.call-update) | async-done | bytes 4194320 | tf_op jit(solution)/shard_map/all_gather | solution.py:243
  143.0 54.8 %all-gather.14.cloned.1.call-done = bf16[2048,2048]{1,0:T(8,128)(2,1)} async-done(((bf16[256,2048]{1,0:T(8,128)(2,1)}), bf16[2048,2048]{1,0:T(8,128)(2,1)}) %all-gather.14.cloned.1.call-update) | async-done | bytes 8388624 | tf_op jit(solution)/shard_map/all_gather | solution.py:239
  197.9 31.6 %multiply_convert_fusion.1 = (bf16[1024,2048]{1,0:T(8,128)(2,1)}, f32[1024,2048]{1,0:T(8,128)}, f32[1024,2048]{1,0:T(8,128)}) fusion(f32[2048]{0:T(1024)S(1)} %bitcast.299, bf16[2048,2048]{1,0:T(8,128)(2,1)} %all-gather.14.cloned.1.call-done, bf16[1,1024,2048]{2,1,0:T(8,128)(2,1)} %all-gather.12.cloned.1.call-done), kind=kOutput, calls=%fused_computation.61 | convolution fusion | flops 8728346624 | bytes 33562624 | tf_op jit(solution)/shard_map/dot_general | solution.py:44
  229.5 50.8 %all-gather.18.cloned.1.call-done = bf16[1,1024,2048]{2,1,0:T(8,128)(2,1)} async-done(((bf16[1,256,2048]{2,1,0:T(8,128)(2,1)}), bf16[1,1024,2048]{2,1,0:T(8,128)(2,1)}) %all-gather.18.cloned.1.call-update) | async-done | bytes 4194320 | tf_op jit(solution)/shard_map/all_gather | solution.py:254
  280.3 54.7 %all-gather.16.cloned.1.call-done = bf16[2048,2048]{1,0:T(8,128)(2,1)} async-done(((bf16[256,2048]{1,0:T(8,128)(2,1)}), bf16[2048,2048]{1,0:T(8,128)(2,1)}) %all-gather.16.cloned.1.call-update) | async-done | bytes 8388624 | tf_op jit(solution)/shard_map/all_gather | solution.py:241
  335.0 19.4 fusion.110
  356.3 12.9 convert_bitcast_fusion
  369.3 14.1 convolution_convert_fusion.1
  383.9 31.2 %all-gather.10.cloned.1.call-done = bf16[2048,2048]{1,0:T(8,128)(2,1)} async-done(((bf16[64,2048]{1,0:T(8,128)(2,1)}), bf16[2048,2048]{1,0:T(8,128)(2,1)}) %all-gather.10.cloned.1.call-update) | async-done | bytes 8388624 | tf_op jit(solution)/shard_map/all_gather | solution.py:188
  415.0 5.7 fusion.88
  422.3 4.7 all-to-all-start.4
  427.0 163.5 %all-gather.8.cloned.1.call-done = bf16[2048,6144]{1,0:T(8,128)(2,1)} async-done(((bf16[64,6144]{1,0:T(8,128)(2,1)}), bf16[2048,6144]{1,0:T(8,128)(2,1)}) %all-gather.8.cloned.1.call-update) | async-done | bytes 25165840 | tf_op jit(solution)/shard_map/all_gather | solution.py:186
  590.5 12.6 fusion.68
  612.8 4.2 all-to-all-start.1
  618.9 53.1 %all-to-all-done.1 = bf16[1,256,16,128]{3,1,0,2:T(8,128)(2,1)} async-done(((bf16[1,256,16,128]{3,1,0,2:T(8,128)(2,1)}), bf16[1,256,16,128]{3,1,0,2:T(8,128)(2,1)}, u32[]{:S(2)}, u32[]{:S(2)}) %all-to-all-start.1) | async-done | bytes 1048608 | tf_op jit(solution)/shard_map/all_to_all | solution.py:219
  672.0 3.9 all-to-all-start
  679.0 33.3 %all-to-all-done = bf16[1,256,16,128]{3,1,0,2:T(8,128)(2,1)S(1)} async-done(((bf16[1,256,16,128]{3,1,0,2:T(8,128)(2,1)}), bf16[1,256,16,128]{3,1,0,2:T(8,128)(2,1)S(1)}, u32[]{:S(2)}, u32[]{:S(2)}) %all-to-all-start) | async-done | bytes 1048608 | tf_op jit(solution)/shard_map/all_to_all | solution.py:216
  712.3 4.3 all-to-all-start.2
  716.6 15.0 convolution_convert_fusion
  736.3 5.7 all-to-all-done.2
  745.4 26.7 %while.31 = (s32[]{:T(128)}, bf16[2,1,512,4,128]{4,2,0,3,1:T(8,128)(2,1)}, f32[2,1,4,512]{3,2,1,0:T(4,128)S(1)}, s32[2]{0:T(128)S(1)}, bf16[1,1024,4,128]{3,1,2,...) while((s32[]{:T(128)}, ...), condition=%wide.region_5.6_spmd.clone, body=%wide.region_2.5_spmd.clone.sunk | while | flops 1099955712 | bytes 35199700 | solution.py:81
  749.7 2.9 fusion.147
  755.1 3.7 fusion.149
  763.1 2.9 fusion.147
  768.4 3.7 fusion.149
  773.2 55.0 %while.32 = (s32[]{:T(128)}, f32[1,1024,4,128]{1,3,2,0:T(8,128)S(1)}, f32[1,1024,4,128]{1,3,2,0:T(8,128)}, bf16[2,1,512,4,128]{4,2,0,3,1:T(8,128)(2,1)}, s32[2]{...) while((s32[]{:T(128)}, ...), condition=%wide.region_9.10_spmd.clone, body=%wide.region_7.9_spmd.clone.sunk | while | flops 2709257728 | bytes 170966912 | solution.py:131
  776.0 2.8 fusion.158
  780.5 3.7 multiply_reduce_fusion.2
  784.3 3.3 copy-done
  790.0 3.8 bitcast_add_fusion.4
  802.9 2.9 fusion.158
  807.5 3.7 multiply_reduce_fusion.2
  811.2 3.5 copy-done
  817.1 3.8 bitcast_add_fusion.4
  824.3 3.9 bitcast_add_fusion.5
  828.2 3.1 copy.149
  831.3 3.5 all-to-all-start.5
  836.5 22.4 %all-to-all-done.5 = bf16[1,1024,4,128]{3,2,0,1:T(4,128)(2,1)S(1)} async-done(((bf16[1,1024,4,128]{3,2,0,1:T(4,128)(2,1)}), bf16[1,1024,4,128]{3,2,0,1:T(4,128)(2,1)S(1)}, u32[]{:S(2)}, u32[]{:S(2)}) %all-to-all-start.5) | async-done | bytes 1048608 | tf_op jit(solution)/shard_map/all_to_all | solution.py:297
  859.9 3.5 all-to-all-start.6
  863.5 14.3 convert_bitcast_fusion.1
  877.8 2.9 copy.154
  880.6 8.0 all-to-all-done.6
  888.6 4.3 all-to-all-start.7
  892.9 3.0 copy.143
  900.6 45.7 %all-to-all-done.7 = bf16[1,1024,4,128]{3,2,0,1:T(4,128)(2,1)} async-done(((bf16[1,1024,4,128]{3,2,0,1:T(4,128)(2,1)}), bf16[1,1024,4,128]{3,2,0,1:T(4,128)(2,1)}, u32[]{:S(2)}, u32[]{:S(2)}) %all-to-all-start.7) | async-done | bytes 1048608 | tf_op jit(solution)/shard_map/all_to_all | solution.py:303
  946.3 3.9 all-to-all-start.3
  958.1 3.4 convert_reduce_fusion
  961.4 4.7 copy.156
  966.1 31.0 %all-to-all-done.3 = bf16[1,1024,4,128]{3,2,0,1:T(4,128)(2,1)S(1)} async-done(((bf16[1,1024,4,128]{3,2,0,1:T(4,128)(2,1)}), bf16[1,1024,4,128]{3,2,0,1:T(4,128)(2,1)S(1)}, u32[]{:S(2)}, u32[]{:S(2)}) %all-to-all-start.3) | async-done | bytes 1048608 | tf_op jit(solution)/shard_map/all_to_all | solution.py:227
  999.8 14.7 fusion.79
  1016.9 3.8 fusion.81
  1020.8 3.4 fusion.86
  1024.3 8.1 fusion.94
  1033.1 21.9 %fusion.103 = f32[2048,6144]{1,0:T(8,128)} fusion(bf16[256,6144]{0,1:T(8,128)(2,1)} %bitcast.282, bf16[1,256,2048]{2,1,0:T(8,128)(2,1)S(1)} %copy-done.4, f32[2048]{0:T(1024)S(1)} %copy-done.31, f32[2048]{0:T(1024)S(1)} %copy-done.29, f32[256]{0:T(256)S(1)} %copy-done.35, f32[256]{0:T(256)S(1)} %copy-done.37), kind=kOutput, calls=%fused_computation.179 | convolution fusion | flops 6445596672 | bytes 54544384 | tf_op jit(solution)/shard_map/dot_general | solution.py:50
  1056.9 13.9 all-reduce.19
  1071.5 2.8 convert_element_type.312
  1074.3 2.8 convert_element_type.315
  1077.1 7.5 fusion.71
  1084.6 62.8 %all-reduce.28.cloned.1.call-done = (f32[6144]{0:T(1024)}, f32[2048]{0:T(1024)}, f32[2048]{0:T(1024)}, f32[2048]{0:T(1024)}, f32[2048]{0:T(1024)}, /*index=5*/f32[2048]{0:T(1024)}) async-done(((f32[6144]{0:T(1024)}, f32[2048]{0:T(1024)}, f32[2048]{0:T(1024)}, f32[2048]{0:T(1024)}, f32[2048]{0:T(1024)}, /*index=5*/f32[2048]{0:T(1024)}), (f32[6144]{0:T(1024)}, f32[2048]{0:T(1024)}, f32[2048]{0:T(1024)}, ...) | async-done | bytes 65552
  1154.5 361.0 %reduce-scatter.13.cloned.1.call-done = f32[64,2048]{1,0:T(8,128)} async-done(((f32[2048,2048]{1,0:T(8,128)}), f32[64,2048]{1,0:T(8,128)}) %reduce-scatter.13.cloned.1.call-update) | async-done | bytes 524304 | tf_op jit(solution)/shard_map/reduce_scatter | solution.py:328
  1515.5 436.4 %reduce-scatter.11.cloned.1.call-done = f32[64,6144]{1,0:T(8,128)} async-done(((f32[2048,6144]{1,0:T(8,128)}), f32[64,6144]{1,0:T(8,128)}) %reduce-scatter.11.cloned.1.call-update) | async-done | bytes 1572880 | tf_op jit(solution)/shard_map/reduce_scatter | solution.py:326
  (259 shorter events, 100.0 us)
Async XLA Ops:
  7.2 135.9 %all-gather.12.cloned.1.call-start = ((), (), s32[]{:S(2)}) async-start(), calls=%async_computation.16 | async-start | bytes 5242880 | tf_op jit(solution)/shard_map/all_gather | solution.py:243
  7.2 56.6 %copy-start.18 = (bf16[1,256,2048]{2,1,0:T(8,128)(2,1)S(1)}, bf16[1,256,2048]{2,1,0:T(8,128)(2,1)}, u32[]{:S(2)}) copy-start(bf16[1,256,2048]{2,1,0:T(8,128)(2,1)} %param.21) | copy-start | bytes 3145732
  8.8 581.7 %copy-start.36 = (f32[256]{0:T(256)}, f32[256]{0:T(256)S(1)}, u32[]{:S(2)}) copy-start(f32[256]{0:T(256)S(1)} %broadcast_multiply_fusion.1) | copy-start | bytes 3076
  10.4 49.2 %copy-start.38 = (f32[256]{0:T(256)}, f32[256]{0:T(256)S(1)}, u32[]{:S(2)}) copy-start(f32[256]{0:T(256)S(1)} %fusion.78) | copy-start | bytes 3076
  10.5 580.0 %copy-start.34 = (f32[256]{0:T(256)}, f32[256]{0:T(256)S(1)}, u32[]{:S(2)}) copy-start(f32[256]{0:T(256)S(1)} %fusion.101) | copy-start | bytes 3076
  59.7 5.4 copy-start.32
  62.4 4.6 copy-start.45
  62.4 135.5 %all-gather.14.cloned.1.call-start = ((), (), s32[]{:S(2)}) async-start(), calls=%async_computation.17 | async-start | bytes 9437184 | tf_op jit(solution)/shard_map/all_gather | solution.py:239
  63.1 217.1 %all-gather.18.cloned.1.call-start = ((), (), s32[]{:S(2)}) async-start(), calls=%async_computation.20 | async-start | bytes 5242880 | tf_op jit(solution)/shard_map/all_gather | solution.py:254
  63.9 3.1 copy-start.40
  65.1 269.8 %all-gather.16.cloned.1.call-start = ((), (), s32[]{:S(2)}) async-start(), calls=%async_computation.18 | async-start | bytes 9437184 | tf_op jit(solution)/shard_map/all_gather | solution.py:241
  65.7 349.3 %all-gather.10.cloned.1.call-start = ((), (), s32[]{:S(2)}) async-start(), calls=%async_computation.15 | async-start | bytes 8650752 | tf_op jit(solution)/shard_map/all_gather | solution.py:188
  66.3 524.2 %all-gather.8.cloned.1.call-start = ((), (), s32[]{:S(2)}) async-start(), calls=%async_computation.14 | async-start | bytes 25952256 | tf_op jit(solution)/shard_map/all_gather | solution.py:186
  66.9 932.8 %reduce-scatter.9.cloned.1.call-start = ((), (), s32[]{:S(2)}) async-start(), calls=%async_computation.21 | async-start | bytes 5242880 | tf_op jit(solution)/shard_map/reduce_scatter | solution.py:260
  369.2 702.3 %reduce-scatter.15.cloned.1.call-start = ((), (), s32[]{:S(2)}) async-start(), calls=%async_computation.24 | async-start | bytes 9437184 | tf_op jit(solution)/shard_map/reduce_scatter | solution.py:267
  383.4 31.6 %copy-start.12 = (bf16[1,256,2048]{2,1,0:T(8,128)(2,1)S(1)}, bf16[1,256,2048]{2,1,0:T(8,128)(2,1)}, u32[]{:S(2)}) copy-start(bf16[1,256,2048]{2,1,0:T(8,128)(2,1)} %fusion.87) | copy-start | bytes 3145732
  383.4 207.1 %copy-start.28 = (f32[2048]{0:T(1024)}, f32[2048]{0:T(1024)S(1)}, u32[]{:S(2)}) copy-start(f32[2048]{0:T(1024)S(1)} %convert_element_type.269) | copy-start | bytes 24580
  383.5 207.1 %copy-start.30 = (f32[2048]{0:T(1024)}, f32[2048]{0:T(1024)S(1)}, u32[]{:S(2)}) copy-start(f32[2048]{0:T(1024)S(1)} %convert_element_type.270) | copy-start | bytes 24580
  383.8 226.1 %copy-start.24 = (f32[256,32]{1,0:T(8,128)}, f32[256,32]{1,0:T(8,128)S(1)}, u32[]{:S(2)}) copy-start(f32[256,32]{1,0:T(8,128)S(1)} %copy.133) | copy-start | bytes 98308
  383.9 226.1 %copy-start.26 = (f32[256,32]{1,0:T(8,128)}, f32[256,32]{1,0:T(8,128)S(1)}, u32[]{:S(2)}) copy-start(f32[256,32]{1,0:T(8,128)S(1)} %copy.134) | copy-start | bytes 98308
  420.8 169.7 %copy-start.3 = (bf16[1,256,2048]{2,1,0:T(8,128)(2,1)S(1)}, bf16[1,256,2048]{2,1,0:T(8,128)(2,1)}, u32[]{:S(2)}) copy-start(bf16[1,256,2048]{2,1,0:T(8,128)(2,1)} %param.19) | copy-start | bytes 3145732
  422.3 190.5 %all-to-all-start.4 = ((bf16[1,256,16,128]{3,1,0,2:T(8,128)(2,1)}), bf16[1,256,16,128]{3,1,0,2:T(8,128)(2,1)}, u32[]{:S(2)}, u32[]{:S(2)}) async-start(bf16[1,256,16,128]{3,1,0,2:T(8,128)(2,1)} %copy.146), calls=%async_computation.5 | async-start | bytes 2097152 | tf_op jit(solution)/shard_map/all_to_all | solution.py:286
  604.2 2.6 copy-start.10
  612.8 59.3 %all-to-all-start.1 = ((bf16[1,256,16,128]{3,1,0,2:T(8,128)(2,1)}), bf16[1,256,16,128]{3,1,0,2:T(8,128)(2,1)}, u32[]{:S(2)}, u32[]{:S(2)}) async-start(bf16[1,256,16,128]{3,1,0,2:T(8,128)(2,1)} %maximum_bitcast_fusion.1), calls=%async_computation.1 | async-start | bytes 2097152 | tf_op jit(solution)/shard_map/all_to_all | solution.py:219
  672.0 40.2 %all-to-all-start = ((bf16[1,256,16,128]{3,1,0,2:T(8,128)(2,1)}), bf16[1,256,16,128]{3,1,0,2:T(8,128)(2,1)S(1)}, u32[]{:S(2)}, u32[]{:S(2)}) async-start(bf16[1,256,16,128]{3,1,0,2:T(8,128)(2,1)} %maximum_bitcast_fusion), calls=%async_computation | async-start | bytes 2097152 | tf_op jit(solution)/shard_map/all_to_all | solution.py:216
  712.2 19.3 copy-start.22
  712.3 29.8 %all-to-all-start.2 = ((bf16[1,256,16,128]{3,1,0,2:T(8,128)(2,1)}), bf16[1,256,16,128]{3,1,0,2:T(8,128)(2,1)}, u32[]{:S(2)}, u32[]{:S(2)}) async-start(bf16[1,256,16,128]{3,1,0,2:T(8,128)(2,1)} %bitcast.288), calls=%async_computation.2 | async-start | bytes 2097152 | tf_op jit(solution)/shard_map/all_to_all | solution.py:222
  716.5 357.7 %reduce-scatter.17.cloned.1.call-start = ((), (), s32[]{:S(2)}) async-start(), calls=%async_computation.25 | async-start | bytes 9437184 | tf_op jit(solution)/shard_map/reduce_scatter | solution.py:273
  731.6 3.7 copy-start.23
  752.7 2.4 copy-start.5
  766.0 2.4 copy-start.5
  776.0 4.6 copy-start.7
  784.3 3.3 copy-start
  790.0 3.9 copy-start.2
  790.0 7.5 copy-start.1
  793.8 4.2 copy-start.6
  802.8 4.7 copy-start.7
  811.2 3.5 copy-start
  817.1 3.9 copy-start.2
  817.1 6.7 copy-start.1
  821.0 3.3 copy-start.6
  831.3 27.6 %all-to-all-start.5 = ((bf16[1,1024,4,128]{3,2,0,1:T(4,128)(2,1)}), bf16[1,1024,4,128]{3,2,0,1:T(4,128)(2,1)S(1)}, u32[]{:S(2)}, u32[]{:S(2)}) async-start(bf16[1,1024,4,128]{3,2,0,1:T(4,128)(2,1)} %copy.149), calls=%async_computation.6 | async-start | bytes 2097152 | tf_op jit(solution)/shard_map/all_to_all | solution.py:297
  859.9 28.8 %all-to-all-start.6 = ((bf16[1,1024,4,128]{3,2,0,1:T(4,128)(2,1)}), bf16[1,1024,4,128]{3,2,0,1:T(4,128)(2,1)S(1)}, u32[]{:S(2)}, u32[]{:S(2)}) async-start(bf16[1,1024,4,128]{3,2,0,1:T(4,128)(2,1)} %copy.152), calls=%async_computation.7 | async-start | bytes 2097152 | tf_op jit(solution)/shard_map/all_to_all | solution.py:300
  863.4 213.6 %reduce-scatter.7.cloned.1.call-start = ((), (), s32[]{:S(2)}) async-start(), calls=%async_computation.19 | async-start | bytes 5242880 | tf_op jit(solution)/shard_map/reduce_scatter | solution.py:247
  877.7 18.2 copy-start.21
  888.6 57.6 %all-to-all-start.7 = ((bf16[1,1024,4,128]{3,2,0,1:T(4,128)(2,1)}), bf16[1,1024,4,128]{3,2,0,1:T(4,128)(2,1)}, u32[]{:S(2)}, u32[]{:S(2)}) async-start(bf16[1,1024,4,128]{3,2,0,1:T(4,128)(2,1)} %copy.154), calls=%async_computation.8 | async-start | bytes 2097152 | tf_op jit(solution)/shard_map/all_to_all | solution.py:303
  900.6 51.2 %copy-start.27 = (f32[256,32]{1,0:T(8,128)S(1)}, f32[256,32]{1,0:T(8,128)}, u32[]{:S(2)}) copy-start(f32[256,32]{1,0:T(8,128)} %copy-done.26) | copy-start | bytes 98308
  946.3 50.8 %all-to-all-start.3 = ((bf16[1,1024,4,128]{3,2,0,1:T(4,128)(2,1)}), bf16[1,1024,4,128]{3,2,0,1:T(4,128)(2,1)S(1)}, u32[]{:S(2)}, u32[]{:S(2)}) async-start(bf16[1,1024,4,128]{3,2,0,1:T(4,128)(2,1)} %copy.143), calls=%async_computation.3 | async-start | bytes 2097152 | tf_op jit(solution)/shard_map/all_to_all | solution.py:227
  950.2 197.1 %all-reduce.28.cloned.1.call-start = ((), (), s32[]{:S(2)}) async-start(), calls=%async_computation.26 | async-start | bytes 131072
  966.1 33.6 %copy-start.4 = (bf16[1,256,2048]{2,1,0:T(8,128)(2,1)S(1)}, bf16[1,256,2048]{2,1,0:T(8,128)(2,1)}, u32[]{:S(2)}) copy-start(bf16[1,256,2048]{2,1,0:T(8,128)(2,1)} %param.19) | copy-start | bytes 3145732
  966.1 33.6 %copy-start.29 = (f32[2048]{0:T(1024)S(1)}, f32[2048]{0:T(1024)}, u32[]{:S(2)}) copy-start(f32[2048]{0:T(1024)} %copy-done.28) | copy-start | bytes 24580
  966.1 33.6 %copy-start.33 = (f32[2048]{0:T(1024)S(1)}, f32[2048]{0:T(1024)}, u32[]{:S(2)}) copy-start(f32[2048]{0:T(1024)} %copy-done.32) | copy-start | bytes 24580
  966.1 33.6 %copy-start.37 = (f32[256]{0:T(256)S(1)}, f32[256]{0:T(256)}, u32[]{:S(2)}) copy-start(f32[256]{0:T(256)} %copy-done.36) | copy-start | bytes 3076
  999.8 17.1 copy-start.39
  999.8 17.1 copy-start.16
  999.8 17.1 copy-start.35
  1014.6 6.2 copy-start.41
  1016.9 3.9 copy-start.11
  1016.9 3.9 copy-start.17
  1016.9 3.9 copy-start.19
  1020.8 3.5 copy-start.13
  1024.2 491.2 %reduce-scatter.13.cloned.1.call-start = ((), (), s32[]{:S(2)}) async-start(), calls=%async_computation.23 | async-start | bytes 17301504 | tf_op jit(solution)/shard_map/reduce_scatter | solution.py:328
  1032.4 919.5 %reduce-scatter.11.cloned.1.call-start = ((), (), s32[]{:S(2)}) async-start(), calls=%async_computation.22 | async-start | bytes 51904512 | tf_op jit(solution)/shard_map/reduce_scatter | solution.py:326
  1148.1 804.3 %copy-start.47 = (f32[64]{0:T(128)}, f32[64]{0:T(128)S(1)}, u32[]{:S(2)}) copy-start(f32[64]{0:T(128)S(1)} %dynamic-slice.16) | copy-start | bytes 772
  (12 other events, 15.7 us)
Sparse Core Ops, SparseCore 0:
  62.5 80.5 all-gather.11
  144.9 52.9 all-gather.13
  199.5 80.7 all-gather.17
  282.0 52.9 all-gather.15
  337.7 77.2 all-gather.9
  417.8 172.6 all-gather.7
  592.8 99.6 reduce-scatter.8
  696.4 88.4 reduce-scatter.14
  788.3 71.2 reduce-scatter.16
  877.9 111.9 reduce-scatter.6
  1024.4 122.9 all-reduce.27
  1150.1 365.3 reduce-scatter.12
  1522.5 429.3 reduce-scatter.10
where the time goes:
time: 1960 us
  waiting for transfers between devices  1480 us (76%)
  matrix products  222 us (11%)
  local copies, waits for them, and re-layouts  76 us (4%)
  blocking collectives  66.9 us (3%)
  other arithmetic  53.9 us (3%)
  starting transfers between devices  32.8 us (2%)
    reduce_scatter x1, waiting for transfers between devices, local(): lax.psum_scatter(in_delta, ('fsdp', 'seq'), scatter_dimension=0, tiled=True)  436 us
    reduce_scatter x1, waiting for transfers between devices, local(): lax.psum_scatter(out_delta, ('fsdp', 'seq'), scatter_dimension=0, tiled=T...  361 us
    all_gather x1, waiting for transfers between devices, local(): lax.all_gather(in_weight, ('fsdp', 'seq'), axis=0, tiled=True)  164 us
    dot_general x4, matrix products, times_transposed(): lax.dot_general(left_side, right_side, (((1,), (1,)), ((), ())), preferre...  71.4 us
    all_gather x1, waiting for transfers between devices, local(): lax.all_gather(second_in, 'seq', axis=1, tiled=True)  66.3 us
    unnamed x14, waiting for transfers between devices  65.2 us
    dot_general x4, matrix products, transposed_times(): lax.dot_general(left_side, right_side, (((0,), (0,)), ((), ())), preferre...  59.1 us
    unnamed x2, blocking collectives  57.1 us
  transfers between devices with their start and end apart: 21, of which 16 were waited for; matrix products, arithmetic and copies ran while one was open for 16% of the time, Pallas kernels for 0%

commit v1 on v0

--- a/solution.py
+++ b/solution.py
@@ -8,6 +8,28 @@
 ROT = 32
 EPSILON = 1e-05
 MASKED_SCORE = -1e30
+
+
+def joined_along(pieces, dim):
+    dims = list(pieces.shape[1:])
+    dims[dim] *= pieces.shape[0]
+    return jnp.moveaxis(pieces, 0, dim).reshape(dims)
+
+
+def collect(shard, axis, dim):
+    size = lax.axis_size(axis)
+    pairs = [(i, (i + 1) % size) for i in range(size)]
+    back = [(b, a) for a, b in pairs]
+    lower, upper = ([], [])
+    for step in range(size - 1):
+        if step % 2 == 0:
+            lower.append(lax.ppermute(lower[-1] if lower else shard, axis, pairs))
+        else:
+            upper.append(lax.ppermute(upper[-1] if upper else shard, axis, back))
+    blocks = jnp.stack([*lower[::-1], shard, *upper])
+    shift = lax.axis_index(axis) - len(lower)
+    blocks = blocks[(jnp.arange(size) - shift) % size]
+    return joined_along(blocks, dim)
 
 
 def layer_norm(values, norm_gain, norm_shift):
@@ -236,7 +258,7 @@
     delta_low = delta_out.astype(jnp.bfloat16)
     delta_rows = delta_low.reshape(row_count, width)
     up_matrix, up_offset, down_matrix = (
-        lax.all_gather(up_weight, "fsdp", axis=0, tiled=True),
+        collect(up_weight, "fsdp", 0),
         lax.all_gather(up_bias, "fsdp", axis=0, tiled=True),
         lax.all_gather(down_weight, "fsdp", axis=0, tiled=True),
     )

time: 1960 us -> 1890 us (0.964)
  waiting for transfers between devices: 1480 us -> 1390 us
    all_gather x1, waiting for transfers between devices: 66.3 us -> 0.01 us  [local(): lax.all_gather(second_in, 'seq', axis=1, tiled=True)]
    ppermute x0 -> x7, waiting for transfers between devices: none -> 63.4 us  [the longest x4 62.1 us: collect(): lower.append(lax.ppermute(lower[-1] if lower else shard, axis, pairs))]
    all_gather x1 -> x0, waiting for transfers between devices: 54.8 us -> none  [local(): lax.all_gather(up_weight, 'fsdp', axis=0, tiled=True)]
    all_to_all x1, waiting for transfers between devices: 53.1 us -> 6.23 us  [local(): lax.all_to_all(turned[1].astype(jnp.bfloat16), 'seq', split_axis=2, conca...]
    all_to_all x1, waiting for transfers between devices: 5.68 us -> 47.4 us  [local(): lax.all_to_all(joined[:, :, 2].astype(jnp.bfloat16), 'seq', split_axis=2,...]
    all_gather x1, waiting for transfers between devices: 50.8 us -> 18.6 us  [local(): lax.all_gather(delta_low, 'seq', axis=1, tiled=True)]
    unnamed x14 -> x13, waiting for transfers between devices: 65.2 us -> 62.3 us
  transfers between devices with their start and end apart: 21 -> 27, of which waited for: 16 -> 18; matrix products, arithmetic and copies ran while one was open for 16% -> 18% of each run, Pallas kernels for 0% -> 0%
where the time goes in v1:
time: 1890 us; the launch traced here: 1880 us
  waiting for transfers between devices  1390 us (74%)
  matrix products  213 us (11%)
  local copies, waits for them, and re-layouts  90.6 us (5%)
  blocking collectives  71.6 us (4%)
  other arithmetic  49.1 us (3%)
  starting transfers between devices  38.4 us (2%)
    reduce_scatter x1, waiting for transfers between devices, local(): lax.psum_scatter(in_delta, ('fsdp', 'seq'), scatter_dimension=0, tiled=True)  436 us
    reduce_scatter x1, waiting for transfers between devices, local(): lax.psum_scatter(out_delta, ('fsdp', 'seq'), scatter_dimension=0, tiled=T...  361 us
    all_gather x1, waiting for transfers between devices, local(): lax.all_gather(in_weight, ('fsdp', 'seq'), axis=0, tiled=True)  165 us
    dot_general x4, matrix products, times_transposed(): lax.dot_general(left_side, right_side, (((1,), (1,)), ((), ())), preferre...  72.3 us
    unnamed x13, waiting for transfers between devices  62.3 us
    ppermute x4, waiting for transfers between devices, collect(): lower.append(lax.ppermute(lower[-1] if lower else shard, axis, pairs))  62.1 us
    dot_general x4, matrix products, transposed_times(): lax.dot_general(left_side, right_side, (((0,), (0,)), ((), ())), preferre...  59.9 us
    unnamed x2, blocking collectives  55.1 us
  transfers between devices with their start and end apart: 27, of which 18 were waited for; matrix products, arithmetic and copies ran while one was open for 18% of the time, Pallas kernels for 0%

profile of v1, /device:TPU:0, one launch (start us, length us, event | category | flops | bytes accessed | tf_op | source)
XLA Modules:
  0.0 1882.0 jit_solution(5119229594335098638)
XLA Ops:
  16.4 43.2 %all-reduce.25 = (bf16[6144]{0:T(1024)(128)(2,1)S(1)}, bf16[2048]{0:T(1024)(128)(2,1)S(1)}, bf16[2048]{0:T(1024)(128)(2,1)S(1)}, bf16[2048]{0:T(1024)(128)(2,1)S...) all-reduce(bf16[6144]{0:T(1024)(128)(2,1)S(1)} %dynamic-update-slic, ...), channel_id=1, replica_groups=mesh['fsdp'=8,'seq'=4] {'fsdp','seq'}, use_global_device_ids=true, to_apply=%add.12 | all-reduce | flops 18432 | bytes 73728
  60.3 2.7 fusion.76
  67.0 15.1 collective-permute-done
  82.1 2.6 collective-permute-start.4
  84.8 23.4 %collective-permute-done.1 = bf16[256,2048]{1,0:T(8,128)(2,1)S(1)} collective-permute-done((bf16[256,2048]{1,0:T(8,128)(2,1)S(1)}, bf16[256,2048]{1,0:T(8,128)(2,1)S(1)}, u32[]{:S(2)}, u32[]{:S(2)}) %collective-permute-start.1) | collective-permute-done | bytes 1048608 | tf_op jit(solution)/shard_map/ppermute | solution.py:26
  110.8 23.6 %collective-permute-done.2 = bf16[256,2048]{1,0:T(8,128)(2,1)} collective-permute-done((bf16[256,2048]{1,0:T(8,128)(2,1)S(1)}, bf16[256,2048]{1,0:T(8,128)(2,1)}, u32[]{:S(2)}, u32[]{:S(2)}) %collective-permute-start.2) | collective-permute-done | bytes 1048608 | tf_op jit(solution)/shard_map/ppermute | solution.py:26
  134.5 16.5 all-gather
  152.6 2.4 bitcast_dynamic-update-slice_fusion.8
  166.3 8.1 gather_fusion
  174.4 31.6 %multiply_convert_fusion.1 = (bf16[1024,2048]{1,0:T(8,128)(2,1)}, f32[1024,2048]{1,0:T(8,128)}, f32[1024,2048]{1,0:T(8,128)}) fusion(f32[2048]{0:T(1024)S(1)} %bitcast.321, bf16[2048,2048]{1,0:T(8,128)(2,1)} %bitcast.304, bf16[1,1024,2048]{2,1,0:T(8,128)(2,1)} %all-gather.11.cloned.1.call-done), kind=kOutput, calls=%fused_computation.62 | convolution fusion | flops 8728346624 | bytes 33562624 | tf_op jit(solution)/shard_map/dot_general | solution.py:66
  206.0 18.6 all-gather.15.cloned.1.call-done
  224.6 54.8 %all-gather.13.cloned.1.call-done = bf16[2048,2048]{1,0:T(8,128)(2,1)} async-done(((bf16[256,2048]{1,0:T(8,128)(2,1)}), bf16[2048,2048]{1,0:T(8,128)(2,1)}) %all-gather.13.cloned.1.call-update) | async-done | bytes 8388624 | tf_op jit(solution)/shard_map/all_gather | solution.py:263
  279.5 21.0 %fusion.112 = (bf16[2048]{0:T(1024)(128)(2,1)}, bf16[1024,2048]{1,0:T(8,128)(2,1)}) fusion(f32[1024,2048]{1,0:T(8,128)} %get-tuple-element.290, bf16[2048,2048]{1,0:T(8,128)(2,1)} %all-gather.13.cloned.1.call-done, bf16[1,1024,2048]{2,1,0:T(8,128)(2,1)} %all-gather.15.cloned.1.call-done, f32[1024,2048]{1,0:T(8,128)} %get-tuple-element.315, ...), kind=kOutput, calls=%fused_computation.199 | convolution fusion | flops 8623486976 | bytes 33566720 | tf_op jit(solution)/shard_map/dot_general | solution.py:66
  300.5 12.2 convert_bitcast_fusion
  312.8 14.5 convolution_convert_fusion
  327.7 31.8 %all-gather.9.cloned.1.call-done = bf16[2048,2048]{1,0:T(8,128)(2,1)} async-done(((bf16[64,2048]{1,0:T(8,128)(2,1)}), bf16[2048,2048]{1,0:T(8,128)(2,1)}) %all-gather.9.cloned.1.call-update) | async-done | bytes 8388624 | tf_op jit(solution)/shard_map/all_gather | solution.py:210
  359.5 5.7 fusion.88
  366.8 3.5 all-to-all-start.4
  370.3 164.8 %all-gather.7.cloned.1.call-done = bf16[2048,6144]{1,0:T(8,128)(2,1)} async-done(((bf16[64,6144]{1,0:T(8,128)(2,1)}), bf16[2048,6144]{1,0:T(8,128)(2,1)}) %all-gather.7.cloned.1.call-update) | async-done | bytes 25165840 | tf_op jit(solution)/shard_map/all_gather | solution.py:208
  535.2 12.6 fusion.68
  551.9 4.4 all-to-all-start.2
  556.3 2.9 copy_bitcast_fusion
  563.9 47.4 %all-to-all-done.2 = bf16[1,256,16,128]{3,1,0,2:T(8,128)(2,1)} async-done(((bf16[1,256,16,128]{3,1,0,2:T(8,128)(2,1)}), bf16[1,256,16,128]{3,1,0,2:T(8,128)(2,1)}, u32[]{:S(2)}, u32[]{:S(2)}) %all-to-all-start.2) | async-done | bytes 1048608 | tf_op jit(solution)/shard_map/all_to_all | solution.py:244
  611.3 4.2 all-to-all-start
  619.1 37.8 %all-to-all-done = bf16[1,256,16,128]{3,1,0,2:T(8,128)(2,1)} async-done(((bf16[1,256,16,128]{3,1,0,2:T(8,128)(2,1)}), bf16[1,256,16,128]{3,1,0,2:T(8,128)(2,1)}, u32[]{:S(2)}, u32[]{:S(2)}) %all-to-all-start) | async-done | bytes 1048608 | tf_op jit(solution)/shard_map/all_to_all | solution.py:238
  656.9 4.2 all-to-all-start.1
  661.2 14.1 convolution_convert_fusion.1
  681.2 6.2 all-to-all-done.1
  690.9 28.6 %while.31 = (s32[]{:T(128)}, bf16[2,1,512,4,128]{4,2,0,3,1:T(8,128)(2,1)}, f32[2,1,4,512]{3,2,1,0:T(4,128)S(1)}, s32[2]{0:T(128)S(1)}, bf16[1,1024,4,128]{3,1,2,...) while((s32[]{:T(128)}, ...), condition=%wide.region_5.6_spmd.clone, body=%wide.region_2.5_spmd.clone.sunk | while | flops 1099955712 | bytes 39393536 | solution.py:103
  695.2 3.3 fusion.149
  700.8 3.3 fusion.151
  709.4 3.3 fusion.149
  712.7 2.4 fusion.150
  715.1 3.3 fusion.151
  720.5 34.5 %while.32 = (s32[]{:T(128)}, f32[1,1024,4,128]{1,3,2,0:T(8,128)S(1)}, f32[1,1024,4,128]{1,3,2,0:T(8,128)}, bf16[2,1,512,4,128]{4,2,0,3,1:T(8,128)(2,1)}, s32[2]{...) while((s32[]{:T(128)}, ...), condition=%wide.region_9.10_spmd.clone, body=%wide.region_7.9_spmd.clone.sunk | while | flops 2709257728 | bytes 116441008 | solution.py:153
  725.3 2.5 fusion.160
  727.8 3.7 multiply_reduce_fusion.2
  742.0 2.6 fusion.160
  744.7 3.7 multiply_reduce_fusion.2
  755.1 3.0 copy.149
  758.1 3.5 all-to-all-start.5
  761.6 3.0 copy.143
  764.6 22.4 %all-to-all-done.5 = bf16[1,1024,4,128]{3,2,0,1:T(4,128)(2,1)S(1)} async-done(((bf16[1,1024,4,128]{3,2,0,1:T(4,128)(2,1)}), bf16[1,1024,4,128]{3,2,0,1:T(4,128)(2,1)S(1)}, u32[]{:S(2)}, u32[]{:S(2)}) %all-to-all-start.5) | async-done | bytes 1048608 | tf_op jit(solution)/shard_map/all_to_all | solution.py:319
  787.0 4.2 all-to-all-start.3
  793.0 23.6 %all-to-all-done.3 = bf16[1,1024,4,128]{3,2,0,1:T(4,128)(2,1)} async-done(((bf16[1,1024,4,128]{3,2,0,1:T(4,128)(2,1)}), bf16[1,1024,4,128]{3,2,0,1:T(4,128)(2,1)}, u32[]{:S(2)}, u32[]{:S(2)}) %all-to-all-start.3) | async-done | bytes 1048608 | tf_op jit(solution)/shard_map/all_to_all | solution.py:249
  816.5 3.5 all-to-all-start.6
  820.1 13.9 convert_bitcast_fusion.1
  837.3 16.4 all-to-all-done.6
  853.7 4.3 all-to-all-start.7
  862.9 47.5 %all-to-all-done.7 = bf16[1,1024,4,128]{3,2,0,1:T(4,128)(2,1)} async-done(((bf16[1,1024,4,128]{3,2,0,1:T(4,128)(2,1)}), bf16[1,1024,4,128]{3,2,0,1:T(4,128)(2,1)}, u32[]{:S(2)}, u32[]{:S(2)}) %all-to-all-start.7) | async-done | bytes 1048608 | tf_op jit(solution)/shard_map/all_to_all | solution.py:325
  919.9 3.1 convert_reduce_fusion
  923.0 4.7 copy.156
  927.8 13.9 fusion.79
  942.5 3.8 fusion.81
  946.3 3.4 fusion.86
  949.8 9.6 fusion.94
  960.1 21.7 %fusion.105 = f32[2048,6144]{1,0:T(8,128)} fusion(bf16[256,6144]{0,1:T(8,128)(2,1)} %bitcast.301, bf16[1,256,2048]{2,1,0:T(8,128)(2,1)S(1)} %copy-done.4, f32[2048]{0:T(1024)S(1)} %copy-done.34, f32[2048]{0:T(1024)S(1)} %copy-done.32, f32[256]{0:T(256)S(1)} %copy-done.38, f32[256]{0:T(256)S(1)} %copy-done.40), kind=kOutput, calls=%fused_computation.195 | convolution fusion | flops 6445596672 | bytes 54544384 | tf_op jit(solution)/shard_map/dot_general | solution.py:72
  983.7 11.9 all-reduce.19
  996.2 2.8 convert_element_type.315
  999.0 2.8 convert_element_type.312
  1001.8 7.5 fusion.71
  1009.4 60.4 %all-reduce.28.cloned.1.call-done = (f32[6144]{0:T(1024)}, f32[2048]{0:T(1024)}, f32[2048]{0:T(1024)}, f32[2048]{0:T(1024)}, f32[2048]{0:T(1024)}, /*index=5*/f32[2048]{0:T(1024)}) async-done(((f32[6144]{0:T(1024)}, f32[2048]{0:T(1024)}, f32[2048]{0:T(1024)}, f32[2048]{0:T(1024)}, f32[2048]{0:T(1024)}, /*index=5*/f32[2048]{0:T(1024)}), (f32[6144]{0:T(1024)}, f32[2048]{0:T(1024)}, f32[2048]{0:T(1024)}, ...) | async-done | bytes 65552
  1076.9 361.2 %reduce-scatter.13.cloned.1.call-done = f32[64,2048]{1,0:T(8,128)} async-done(((f32[2048,2048]{1,0:T(8,128)}), f32[64,2048]{1,0:T(8,128)}) %reduce-scatter.13.cloned.1.call-update) | async-done | bytes 524304 | tf_op jit(solution)/shard_map/reduce_scatter | solution.py:350
  1438.1 436.3 %reduce-scatter.11.cloned.1.call-done = f32[64,6144]{1,0:T(8,128)} async-done(((f32[2048,6144]{1,0:T(8,128)}), f32[64,6144]{1,0:T(8,128)}) %reduce-scatter.11.cloned.1.call-update) | async-done | bytes 1572880 | tf_op jit(solution)/shard_map/reduce_scatter | solution.py:348
  (291 shorter events, 109.9 us)
Async XLA Ops:
  7.2 56.6 %copy-start.14 = (bf16[1,256,2048]{2,1,0:T(8,128)(2,1)S(1)}, bf16[1,256,2048]{2,1,0:T(8,128)(2,1)}, u32[]{:S(2)}) copy-start(bf16[1,256,2048]{2,1,0:T(8,128)(2,1)} %param.21) | copy-start | bytes 3145732
  7.2 167.2 %all-gather.11.cloned.1.call-start = ((), (), s32[]{:S(2)}) async-start(), calls=%async_computation.16 | async-start | bytes 5242880 | tf_op jit(solution)/shard_map/all_gather | solution.py:265
  8.8 526.4 %copy-start.39 = (f32[256]{0:T(256)}, f32[256]{0:T(256)S(1)}, u32[]{:S(2)}) copy-start(f32[256]{0:T(256)S(1)} %broadcast_multiply_fusion.1) | copy-start | bytes 3076
  10.4 4.3 copy-start.41
  10.4 524.7 %copy-start.37 = (f32[256]{0:T(256)}, f32[256]{0:T(256)S(1)}, u32[]{:S(2)}) copy-start(f32[256]{0:T(256)S(1)} %fusion.101) | copy-start | bytes 3076
  60.3 6.7 copy-start.28
  60.3 74.2 %copy-start.48 = (bf16[256]{0:T(256)(128)(2,1)S(1)}, bf16[256]{0:T(256)(128)(2,1)}, u32[]{:S(2)}) copy-start(bf16[256]{0:T(256)(128)(2,1)} %param.27) | copy-start | bytes 1540
  63.0 161.6 %all-gather.15.cloned.1.call-start = ((), (), s32[]{:S(2)}) async-start(), calls=%async_computation.19 | async-start | bytes 5242880 | tf_op jit(solution)/shard_map/all_gather | solution.py:276
  63.8 70.7 %copy-start.43 = (pred[256]{0:T(512)(128)(4,1)}, pred[256]{0:T(512)(128)(4,1)S(1)}, u32[]{:S(2)}) copy-start(pred[256]{0:T(512)(128)(4,1)S(1)} %fusion.100) | copy-start | bytes 772
  65.0 214.4 %all-gather.13.cloned.1.call-start = ((), (), s32[]{:S(2)}) async-start(), calls=%async_computation.17 | async-start | bytes 9437184 | tf_op jit(solution)/shard_map/all_gather | solution.py:263
  65.7 293.8 %all-gather.9.cloned.1.call-start = ((), (), s32[]{:S(2)}) async-start(), calls=%async_computation.15 | async-start | bytes 8650752 | tf_op jit(solution)/shard_map/all_gather | solution.py:210
  66.3 468.9 %all-gather.7.cloned.1.call-start = ((), (), s32[]{:S(2)}) async-start(), calls=%async_computation.14 | async-start | bytes 25952256 | tf_op jit(solution)/shard_map/all_gather | solution.py:208
  66.9 860.9 %reduce-scatter.9.cloned.1.call-start = ((), (), s32[]{:S(2)}) async-start(), calls=%async_computation.20 | async-start | bytes 5242880 | tf_op jit(solution)/shard_map/reduce_scatter | solution.py:282
  67.0 15.2 collective-permute-start
  82.1 26.0 %collective-permute-start.1 = (bf16[256,2048]{1,0:T(8,128)(2,1)S(1)}, bf16[256,2048]{1,0:T(8,128)(2,1)S(1)}, u32[]{:S(2)}, u32[]{:S(2)}) collective-permute-start(bf16[256,2048]{1,0:T(8,128)(2,1)S(1)} %collective-permute-done), channel_id=1, source_target_pairs={{0,4},{4,8},{8,12},{12,16},{16,20},{20,24},{24,28},{28,0},{1,5},{5... | collective-permute-start | bytes 3145736 | tf_op jit(solution)/shard_map/ppermute | solution.py:26
  82.1 26.0 %collective-permute-start.4 = (bf16[256,2048]{1,0:T(8,128)(2,1)S(1)}, bf16[256,2048]{1,0:T(8,128)(2,1)S(1)}, u32[]{:S(2)}, u32[]{:S(2)}) collective-permute-start(bf16[256,2048]{1,0:T(8,128)(2,1)S(1)} %copy-done.28), channel_id=1, source_target_pairs={{4,0},{8,4},{12,8},{16,12},{20,16},{24,20},{28,24},{0,28},{5,1},{9... | collective-permute-start | bytes 3145736 | tf_op jit(solution)/shard_map/ppermute | solution.py:28
  108.2 26.3 %collective-permute-start.2 = (bf16[256,2048]{1,0:T(8,128)(2,1)S(1)}, bf16[256,2048]{1,0:T(8,128)(2,1)}, u32[]{:S(2)}, u32[]{:S(2)}) collective-permute-start(bf16[256,2048]{1,0:T(8,128)(2,1)S(1)} %collective-permute-done.1), channel_id=1, source_target_pairs={{0,4},{4,8},{8,12},{12,16},{16,20},{20,24},{24,28},{28,0},{1,5},{5... | collective-permute-start | bytes 3145736 | tf_op jit(solution)/shard_map/ppermute | solution.py:26
  109.1 41.9 %collective-permute-start.5 = (bf16[256,2048]{1,0:T(8,128)(2,1)S(1)}, bf16[256,2048]{1,0:T(8,128)(2,1)}, u32[]{:S(2)}, u32[]{:S(2)}) collective-permute-start(bf16[256,2048]{1,0:T(8,128)(2,1)S(1)} %collective-permute-done.4), channel_id=1, source_target_pairs={{4,0},{8,4},{12,8},{16,12},{20,16},{24,20},{28,24},{0,28},{5,1},{9... | collective-permute-start | bytes 3145736 | tf_op jit(solution)/shard_map/ppermute | solution.py:28
  134.5 18.2 collective-permute-start.3
  151.0 6.4 copy-start.30
  151.1 14.2 collective-permute-start.6
  279.5 21.1 %copy-start.12 = (bf16[8,256,2048]{2,1,0:T(8,128)(2,1)S(1)}, bf16[8,256,2048]{2,1,0:T(8,128)(2,1)}, u32[]{:S(2)}) copy-start(bf16[8,256,2048]{2,1,0:T(8,128)(2,1)} %gather_fusion) | copy-start | bytes 25165828
  312.7 683.5 %reduce-scatter.17.cloned.1.call-start = ((), (), s32[]{:S(2)}) async-start(), calls=%async_computation.24 | async-start | bytes 9437184 | tf_op jit(solution)/shard_map/reduce_scatter | solution.py:295
  327.3 32.3 %copy-start.11 = (bf16[1,256,2048]{2,1,0:T(8,128)(2,1)S(1)}, bf16[1,256,2048]{2,1,0:T(8,128)(2,1)}, u32[]{:S(2)}) copy-start(bf16[1,256,2048]{2,1,0:T(8,128)(2,1)} %fusion.87) | copy-start | bytes 3145732
  327.3 207.9 %copy-start.31 = (f32[2048]{0:T(1024)}, f32[2048]{0:T(1024)S(1)}, u32[]{:S(2)}) copy-start(f32[2048]{0:T(1024)S(1)} %convert_element_type.269) | copy-start | bytes 24580
  327.3 207.9 %copy-start.33 = (f32[2048]{0:T(1024)}, f32[2048]{0:T(1024)S(1)}, u32[]{:S(2)}) copy-start(f32[2048]{0:T(1024)S(1)} %convert_element_type.270) | copy-start | bytes 24580
  327.6 233.4 %copy-start.24 = (f32[256,32]{1,0:T(8,128)}, f32[256,32]{1,0:T(8,128)S(1)}, u32[]{:S(2)}) copy-start(f32[256,32]{1,0:T(8,128)S(1)} %copy.133) | copy-start | bytes 98308
  327.7 233.3 %copy-start.26 = (f32[256,32]{1,0:T(8,128)}, f32[256,32]{1,0:T(8,128)S(1)}, u32[]{:S(2)}) copy-start(f32[256,32]{1,0:T(8,128)S(1)} %copy.134) | copy-start | bytes 98308
  365.3 169.9 %copy-start.3 = (bf16[1,256,2048]{2,1,0:T(8,128)(2,1)S(1)}, bf16[1,256,2048]{2,1,0:T(8,128)(2,1)}, u32[]{:S(2)}) copy-start(bf16[1,256,2048]{2,1,0:T(8,128)(2,1)} %param.19) | copy-start | bytes 3145732
  366.8 185.1 %all-to-all-start.4 = ((bf16[1,256,16,128]{3,1,0,2:T(8,128)(2,1)}), bf16[1,256,16,128]{3,1,0,2:T(8,128)(2,1)S(1)}, u32[]{:S(2)}, u32[]{:S(2)}) async-start(bf16[1,256,16,128]{3,1,0,2:T(8,128)(2,1)} %copy.146), calls=%async_computation.5 | async-start | bytes 2097152 | tf_op jit(solution)/shard_map/all_to_all | solution.py:308
  551.9 7.3 copy-start.16
  551.9 59.4 %all-to-all-start.2 = ((bf16[1,256,16,128]{3,1,0,2:T(8,128)(2,1)}), bf16[1,256,16,128]{3,1,0,2:T(8,128)(2,1)}, u32[]{:S(2)}, u32[]{:S(2)}) async-start(bf16[1,256,16,128]{3,1,0,2:T(8,128)(2,1)} %bitcast.309), calls=%async_computation.2 | async-start | bytes 2097152 | tf_op jit(solution)/shard_map/all_to_all | solution.py:244
  611.3 45.6 %all-to-all-start = ((bf16[1,256,16,128]{3,1,0,2:T(8,128)(2,1)}), bf16[1,256,16,128]{3,1,0,2:T(8,128)(2,1)}, u32[]{:S(2)}, u32[]{:S(2)}) async-start(bf16[1,256,16,128]{3,1,0,2:T(8,128)(2,1)} %maximum_bitcast_fusion), calls=%async_computation | async-start | bytes 2097152 | tf_op jit(solution)/shard_map/all_to_all | solution.py:238
  656.9 30.6 %all-to-all-start.1 = ((bf16[1,256,16,128]{3,1,0,2:T(8,128)(2,1)}), bf16[1,256,16,128]{3,1,0,2:T(8,128)(2,1)}, u32[]{:S(2)}, u32[]{:S(2)}) async-start(bf16[1,256,16,128]{3,1,0,2:T(8,128)(2,1)} %maximum_bitcast_fusion.1), calls=%async_computation.1 | async-start | bytes 2097152 | tf_op jit(solution)/shard_map/all_to_all | solution.py:241
  661.1 337.9 %reduce-scatter.15.cloned.1.call-start = ((), (), s32[]{:S(2)}) async-start(), calls=%async_computation.23 | async-start | bytes 9437184 | tf_op jit(solution)/shard_map/reduce_scatter | solution.py:289
  725.2 2.5 copy-start.6
  725.2 2.5 copy-start.8
  734.8 2.9 copy-start.1
  742.0 2.7 copy-start.6
  742.0 2.6 copy-start.8
  752.2 2.9 copy-start.1
  758.1 28.9 %all-to-all-start.5 = ((bf16[1,1024,4,128]{3,2,0,1:T(4,128)(2,1)}), bf16[1,1024,4,128]{3,2,0,1:T(4,128)(2,1)S(1)}, u32[]{:S(2)}, u32[]{:S(2)}) async-start(bf16[1,1024,4,128]{3,2,0,1:T(4,128)(2,1)} %copy.149), calls=%async_computation.6 | async-start | bytes 2097152 | tf_op jit(solution)/shard_map/all_to_all | solution.py:319
  787.0 29.5 %copy-start.18 = (bf16[1,1024,4,128]{3,2,0,1:T(4,128)(2,1)}, bf16[1,1024,4,128]{3,2,0,1:T(4,128)(2,1)S(1)}, u32[]{:S(2)}) copy-start(bf16[1,1024,4,128]{3,2,0,1:T(4,128)(2,1)S(1)} %all-to-all-done.5) | copy-start | bytes 3145732
  787.0 29.5 %all-to-all-start.3 = ((bf16[1,1024,4,128]{3,2,0,1:T(4,128)(2,1)}), bf16[1,1024,4,128]{3,2,0,1:T(4,128)(2,1)}, u32[]{:S(2)}, u32[]{:S(2)}) async-start(bf16[1,1024,4,128]{3,2,0,1:T(4,128)(2,1)} %copy.143), calls=%async_computation.3 | async-start | bytes 2097152 | tf_op jit(solution)/shard_map/all_to_all | solution.py:249
  816.5 37.1 %all-to-all-start.6 = ((bf16[1,1024,4,128]{3,2,0,1:T(4,128)(2,1)}), bf16[1,1024,4,128]{3,2,0,1:T(4,128)(2,1)S(1)}, u32[]{:S(2)}, u32[]{:S(2)}) async-start(bf16[1,1024,4,128]{3,2,0,1:T(4,128)(2,1)} %copy.152), calls=%async_computation.7 | async-start | bytes 2097152 | tf_op jit(solution)/shard_map/all_to_all | solution.py:322
  820.1 181.8 %reduce-scatter.7.cloned.1.call-start = ((), (), s32[]{:S(2)}) async-start(), calls=%async_computation.18 | async-start | bytes 5242880 | tf_op jit(solution)/shard_map/reduce_scatter | solution.py:269
  837.3 23.6 %copy-start.19 = (bf16[1,1024,4,128]{3,2,0,1:T(4,128)(2,1)S(1)}, bf16[1,1024,4,128]{3,2,0,1:T(4,128)(2,1)}, u32[]{:S(2)}) copy-start(bf16[1,1024,4,128]{3,2,0,1:T(4,128)(2,1)} %copy-done.18) | copy-start | bytes 3145732
  853.7 56.8 %all-to-all-start.7 = ((bf16[1,1024,4,128]{3,2,0,1:T(4,128)(2,1)}), bf16[1,1024,4,128]{3,2,0,1:T(4,128)(2,1)}, u32[]{:S(2)}, u32[]{:S(2)}) async-start(bf16[1,1024,4,128]{3,2,0,1:T(4,128)(2,1)} %copy.154), calls=%async_computation.8 | async-start | bytes 2097152 | tf_op jit(solution)/shard_map/all_to_all | solution.py:325
  857.9 211.8 %all-reduce.28.cloned.1.call-start = ((), (), s32[]{:S(2)}) async-start(), calls=%async_computation.25 | async-start | bytes 131072
  911.9 3.0 copy-start.9
  911.9 3.0 copy-start.27
  923.0 4.7 copy-start.4
  923.0 4.8 copy-start.32
  923.0 4.8 copy-start.36
  923.0 4.8 copy-start.40
  927.8 14.6 copy-start.42
  927.8 14.7 copy-start.38
  941.7 4.6 copy-start.44
  942.4 3.9 copy-start.13
  942.4 3.9 copy-start.15
  949.8 488.3 %reduce-scatter.13.cloned.1.call-start = ((), (), s32[]{:S(2)}) async-start(), calls=%async_computation.22 | async-start | bytes 17301504 | tf_op jit(solution)/shard_map/reduce_scatter | solution.py:350
  959.5 914.9 %reduce-scatter.11.cloned.1.call-start = ((), (), s32[]{:S(2)}) async-start(), calls=%async_computation.21 | async-start | bytes 51904512 | tf_op jit(solution)/shard_map/reduce_scatter | solution.py:348
  981.8 20.0 %copy-start.10 = (bf16[1,256,4,4,128]{1,4,3,2,0:T(8,128)(2,1)S(1)}, bf16[1,256,4,4,128]{1,4,3,2,0:T(8,128)(2,1)}, u32[]{:S(2)}) copy-start(bf16[1,256,4,4,128]{1,4,3,2,0:T(8,128)(2,1)} %copy.145) | copy-start | bytes 3145732
  1070.5 804.4 %copy-start.50 = (f32[64]{0:T(128)}, f32[64]{0:T(128)S(1)}, u32[]{:S(2)}) copy-start(f32[64]{0:T(128)S(1)} %dynamic-slice.16) | copy-start | bytes 772
  (23 other events, 33.2 us)
Sparse Core Ops, SparseCore 0:
  63.2 80.5 all-gather.10
  145.3 79.2 all-gather.14
  226.5 52.9 all-gather.12
  282.2 77.2 all-gather.8
  362.3 172.8 all-gather.6
  537.3 101.5 reduce-scatter.8
  642.8 88.5 reduce-scatter.16
  734.9 71.2 reduce-scatter.14
  834.1 96.7 reduce-scatter.6
  949.9 119.8 all-reduce.27
  1072.6 365.3 reduce-scatter.12
  1444.9 429.4 reduce-scatter.10
